TPU v7x, 32 devices: a whole 2x2x4 slice. The times are simulated.
32 devices in a mesh: row: 4 (over y, x), col: 8 (over z, core).
Axes of the slice: x: 2, y: 2, z: 4, core: 2. Of those that a mesh axis runs over, the one named last changes fastest.
Arguments:
- boundary_start: float32 [16384, 128], P('row'), may hold values from -6 to 6
- volume_start: float32 [256, 512, 128], P(('row', 'col')), may hold values from -6 to 6
- diag_part: float32 [16384], P(('row', 'col')), may hold values from 1 to 2
- incident: float32 [16384, 128], P(('row', 'col')), may hold values from -6 to 6
- kernel: float32 [16384, 16384], P('row', 'col'), may hold values from -0.015625 to 0.015625
- elem_mats: float32 [256, 512, 512], P(('row', 'col')), may hold values from -0.078125 to 0.078125
- trace_owner: int32 [16384, 1], replicated, may hold values from 0 to 31; in each aligned block of 512 rows (0 to 511, 512 to 1023, ...) at most 32 rows name the same one
- trace_slot: int32 [16384], replicated, may hold values from 0 to 4095
- return_owner: int32 [16384, 1], replicated, may hold values from 0 to 31; in each aligned block of 512 rows (0 to 511, 512 to 1023, ...) at most 32 rows name the same one
- return_slot: int32 [16384], replicated, may hold values from 0 to 4095
- face_match: int32 [256, 64], P(('row', 'col')), may hold values from 0 to 63, each once within a row
Outputs:
- boundary_final: float32 [16384, 128], P('row')
- volume_final: float32 [256, 512, 128], P(('row', 'col'))
Inputs may be any that keep to these rules, and one draw needn't show every extreme that they name: `trace_owner`: in each aligned block of 512 boundary rows (the rows of one device), no device is named more than 32 times; some device is named exactly 32 times in some block. `return_owner`: in each aligned block of 512 boundary rows (the rows of one device), no device is named more than 32 times; some device is named exactly 32 times in some block. `face_match`: each row is a permutation of 0 to 63.
All inputs are finite; a program needn't handle non-finite values.
Results may differ from a plain program's by a relative error of at most 0.0001.
Values sent between devices are 32-bit elements; how exact they have to be, the bound alone decides.
A program may use at most 128 MiB of HBM per device.

v0:
```python
import jax
import jax.numpy as jnp
from jax import lax
from jax.sharding import PartitionSpec as P

ITERS = 3
boundary_step = 0.5
volume_step = 0.6
face_weight = 0.5


def passed_along(block, axis, distance):
    devices = range(lax.axis_size(axis))
    route = [(i - distance, i) for i in devices if i - distance in devices]
    return lax.ppermute(block, axis, route)


def spread(block, axis, holder):
    block = jnp.where(lax.axis_index(axis) == holder, block, jnp.zeros_like(block))
    return lax.psum(block, axis)


def slot_rank(owners):
    row_total = owners.shape[0]
    same_owner = owners[:, None] == owners[None, :]
    positions = jnp.arange(row_total, dtype=jnp.int32)
    earlier = positions[None, :] < positions[:, None]
    return jnp.sum((same_owner & earlier).astype(jnp.int32), axis=1)


def send_plan(owners, rank_rows, devices, capacity):
    positions = jnp.arange(owners.shape[0], dtype=jnp.int32)
    targets = jnp.arange(devices, dtype=jnp.int32)
    places = jnp.arange(capacity, dtype=jnp.int32)
    select = (owners[None, None, :] == targets[:, None, None]) & (
        rank_rows[None, None, :] == places[None, :, None]
    )
    index = jnp.sum(jnp.where(select, positions[None, None, :], 0), axis=2)
    valid_slot = jnp.any(select, axis=2)
    return (index, valid_slot)


def block_plan(owner_blocks, slot_blocks, device_self, capacity):
    mine_rows = owner_blocks == device_self
    rank_rows = jnp.cumsum(mine_rows.astype(jnp.int32), axis=1) - 1
    places = jnp.arange(capacity, dtype=jnp.int32)
    select = mine_rows[:, None, :] & (rank_rows[:, None, :] == places[None, :, None])
    index = jnp.sum(jnp.where(select, slot_blocks[:, None, :], 0), axis=2)
    valid_slot = jnp.any(select, axis=2)
    return (index, valid_slot)


def shards(
    boundary_start,
    volume_start,
    diag_part,
    incident,
    kernel,
    elem_mats,
    trace_owner,
    trace_slot,
    return_owner,
    return_slot,
    face_match,
):
    highest = lax.Precision.HIGHEST
    devices = lax.axis_size(("row", "col"))
    row_devices = lax.axis_size("row")
    col_devices = lax.axis_size("col")
    device_self = lax.axis_index(("row", "col"))
    col_index = lax.axis_index("col")
    total_rows = trace_slot.shape[0]
    share_rows = total_rows // devices
    capacity = max(2, 2 * share_rows // devices)
    panel_length = total_rows // col_devices
    per_panel = col_devices // row_devices
    elem_count, node_count, columns = volume_start.shape
    face_count = face_match.shape[1]
    trace_blocks = trace_owner[:, 0].reshape(devices, share_rows)
    trace_slots = trace_slot.reshape(devices, share_rows)
    return_blocks = return_owner[:, 0].reshape(devices, share_rows)
    return_slots = return_slot.reshape(devices, share_rows)
    trace_send, trace_send_ok = block_plan(trace_blocks, trace_slots, device_self, capacity)
    own_trace = lax.dynamic_index_in_dim(trace_blocks, device_self, 0, keepdims=False)
    trace_pick = own_trace * capacity + slot_rank(own_trace)
    own_return = lax.dynamic_index_in_dim(return_blocks, device_self, 0, keepdims=False)
    flux_send, flux_send_ok = send_plan(own_return, slot_rank(own_return), devices, capacity)
    flux_take, flux_take_ok = block_plan(return_blocks, return_slots, device_self, capacity)
    panel_current = boundary_start
    volume_field = volume_start
    for sweep_index in range(ITERS):
        share_current = lax.dynamic_slice_in_dim(
            panel_current, col_index * share_rows, share_rows, 0
        )
        volume_flat = volume_field.reshape(elem_count * node_count, columns)
        outgoing = jnp.where(trace_send_ok[:, :, None], volume_flat[trace_send], 0.0)
        arrived = lax.all_to_all(outgoing, ("row", "col"), split_axis=0, concat_axis=0, tiled=True)
        traced = arrived.reshape(devices * capacity, columns)[trace_pick]
        leaving = jnp.where(flux_send_ok[:, :, None], share_current[flux_send], 0.0)
        landed = lax.all_to_all(leaving, ("row", "col"), split_axis=0, concat_axis=0, tiled=True)
        landed_rows = jnp.where(flux_take_ok[:, :, None], landed, 0.0).reshape(
            devices * capacity, columns
        )
        flux_field = (
            jnp.zeros_like(volume_flat)
            .at[flux_take.reshape(-1)]
            .add(landed_rows)
            .reshape(volume_field.shape)
        )
        lower_faces = passed_along(volume_field[:, node_count - face_count :, :], ("row", "col"), 1)
        matched = jax.vmap(lambda face_rows, face_order: face_rows[face_order])(
            lower_faces, face_match
        )
        half_panel = lax.dynamic_slice_in_dim(
            panel_current, col_index % per_panel * panel_length, panel_length, 0
        )
        column_values = spread(half_panel, "row", col_index // per_panel)
        local_term = diag_part[:, None] * share_current - incident - traced
        partial_value = jnp.dot(
            kernel, column_values, precision=highest, preferred_element_type=jnp.float32
        )
        row_start = col_index * share_rows
        own_part = lax.dynamic_slice_in_dim(partial_value, row_start, share_rows, 0) + local_term
        partial_value = lax.dynamic_update_slice_in_dim(partial_value, own_part, row_start, 0)
        residual = lax.psum(partial_value, "col")
        panel_current = panel_current - boundary_step * residual
        applied = jnp.einsum("enm,emr->enr", elem_mats, volume_field, precision=highest)
        updated = volume_field - volume_step * (volume_field + applied - flux_field)
        volume_field = updated.at[:, :face_count, :].add(volume_step * face_weight * matched)
    return (panel_current, volume_field)


def solution(mesh):
    placed = (
        P("row", None),
        P(("row", "col"), None, None),
        P(("row", "col")),
        P(("row", "col"), None),
        P("row", "col"),
        P(("row", "col"), None, None),
        P(),
        P(),
        P(),
        P(),
        P(("row", "col"), None),
    )
    return jax.shard_map(
        shards,
        mesh=mesh,
        in_specs=placed,
        out_specs=(P("row", None), P(("row", "col"), None, None)),
        check_vma=False,
    )
```

profile of v0, /device:TPU:0, one launch (start us, length us, event | category | flops | bytes accessed | tf_op | source)
XLA Modules:
  0.0 601.1 jit_solution(13699476681869330466)
XLA Ops:
  20.9 7.3 %all-to-all-start = ((f32[32,32,128]{2,1,0:T(8,128)}), f32[32,32,128]{2,1,0:T(8,128)S(1)}, u32[]{:S(2)}, u32[]{:S(2)}) async-start(f32[32,32,128]{2,1,0:T(8,128)} %broadcast_select_fusion.8), calls=%async_computation | async-start | bytes 1048576 | tf_op jit(solution)/shard_map/all_to_all | solution.py:97
  36.1 8.7 %all-to-all-done = f32[32,32,128]{2,1,0:T(8,128)S(1)} async-done(((f32[32,32,128]{2,1,0:T(8,128)}), f32[32,32,128]{2,1,0:T(8,128)S(1)}, u32[]{:S(2)}, u32[]{:S(2)}) %all-to-all-start) | async-done | bytes 524320 | tf_op jit(solution)/shard_map/all_to_all | solution.py:97
  46.0 23.2 %all-reduce.7.cloned.1.call-done = f32[2048,128]{0,1:T(8,128)} async-done(((f32[2048,128]{0,1:T(8,128)}), f32[2048,128]{0,1:T(8,128)}) %all-reduce.7.cloned.1.call-update) | async-done | bytes 1048592 | tf_op jit(solution)/shard_map/psum | solution.py:20
  69.2 38.4 %fusion.29 = f32[128,4096]{1,0:T(8,128)S(1)} fusion(f32[2048,128]{0,1:T(8,128)} %all-reduce.7.cloned.1.call-done, f32[4096,2048]{1,0:T(8,128)} %param.21), kind=kOutput, calls=%fused_computation.106 | convolution fusion | flops 12884901888 | bytes 36700160 | tf_op jit(solution)/shard_map/dot_general | solution.py:119
  114.6 4.6 all-to-all-start.1
  124.7 10.8 %all-to-all-done.1 = f32[32,32,128]{2,1,0:T(8,128)S(1)} async-done(((f32[32,32,128]{2,1,0:T(8,128)}), f32[32,32,128]{2,1,0:T(8,128)S(1)}, u32[]{:S(2)}, u32[]{:S(2)}) %all-to-all-start.1) | async-done | bytes 524320 | tf_op jit(solution)/shard_map/all_to_all | solution.py:100
  135.7 8.0 %scatter_custom_fusion = f32[4096,128]{1,0:T(8,128)} fusion(s32[1024]{0:T(1024)S(1)} %bitcast.132, f32[1024,128]{1,0:T(8,128)S(1)} %bitcast.123, f32[]{:T(128)} %constant.143.clone.1), kind=kCustom, calls=%fused_computation.44 | custom fusion | flops 131072 | bytes 2097156 | tf_op jit(solution)/shard_map/scatter-add | solution.py:107
  143.7 11.2 %multiply_subtract_fusion.2 = f32[8,512,128]{2,1,0:T(8,128)S(1)} fusion(f32[8,512,128]{2,1,0:T(8,128)} %param.18, f32[8,512,128]{2,1,0:T(8,128)} %bitcast.112, f32[8,512,512]{2,1,0:T(8,128)} %param.22), kind=kOutput, calls=%fused_computation.28 | convolution fusion | flops 3223322624 | bytes 14680064 | tf_op jit(solution)/shard_map/enm,emr->enr/dot_general | solution.py:127
  157.8 33.4 %all-reduce.9.cloned.1.call-done = f32[4096,128]{0,1:T(8,128)} async-done(((f32[4096,128]{0,1:T(8,128)}), f32[4096,128]{0,1:T(8,128)}) %all-reduce.9.cloned.1.call-update) | async-done | bytes 2097168 | tf_op jit(solution)/shard_map/psum | solution.py:125
  196.2 20.6 %all_to_all.30 = f32[32,32,128]{2,1,0:T(8,128)S(1)} all-to-all(f32[32,32,128]{2,1,0:T(8,128)S(1)} %broadcast_select_fusion.5), channel_id=1, replica_groups=mesh['row'=4,'col'=8] {'row','col'}, dimensions={0} | all-to-all | bytes 1048576 | tf_op jit(solution)/shard_map/all_to_all | solution.py:97
  218.1 35.8 %all-reduce.11.cloned.1.call-done = f32[2048,128]{0,1:T(8,128)} async-done(((f32[2048,128]{0,1:T(8,128)}), f32[2048,128]{0,1:T(8,128)}) %all-reduce.11.cloned.1.call-update) | async-done | bytes 1048592 | tf_op jit(solution)/shard_map/psum | solution.py:20
  253.9 39.2 %fusion.30 = f32[128,4096]{1,0:T(8,128)} fusion(f32[2048,128]{0,1:T(8,128)} %all-reduce.11.cloned.1.call-done, f32[4096,2048]{1,0:T(8,128)} %param.21), kind=kOutput, calls=%fused_computation.107 | convolution fusion | flops 12884901888 | bytes 36700160 | tf_op jit(solution)/shard_map/dot_general | solution.py:119
  312.8 9.4 %all-to-all-done.3 = f32[32,32,128]{2,1,0:T(8,128)S(1)} async-done(((f32[32,32,128]{2,1,0:T(8,128)}), f32[32,32,128]{2,1,0:T(8,128)S(1)}, u32[]{:S(2)}, u32[]{:S(2)}) %all-to-all-start.3) | async-done | bytes 524320 | tf_op jit(solution)/shard_map/all_to_all | solution.py:100
  322.4 8.1 %scatter_custom_fusion.1 = f32[4096,128]{1,0:T(8,128)} fusion(s32[1024]{0:T(1024)S(1)} %bitcast.133, f32[1024,128]{1,0:T(8,128)S(1)} %bitcast.124, f32[]{:T(128)} %constant.143.clone.1), kind=kCustom, calls=%fused_computation.42 | custom fusion | flops 131072 | bytes 2097156 | tf_op jit(solution)/shard_map/scatter-add | solution.py:107
  330.6 10.9 %fusion.6 = f32[8,512,128]{2,1,0:T(8,128)S(1)} fusion(f32[8,512,128]{2,1,0:T(8,128)} %copy-done, f32[8,512,128]{2,1,0:T(8,128)} %bitcast.111, f32[8,512,512]{2,1,0:T(8,128)} %param.22), kind=kOutput, calls=%fused_computation.25 | convolution fusion | flops 3223322624 | bytes 14680064 | tf_op jit(solution)/shard_map/enm,emr->enr/dot_general | solution.py:127
  344.4 46.2 %all-reduce.13.cloned.1.call-done = f32[4096,128]{0,1:T(8,128)} async-done(((f32[4096,128]{0,1:T(8,128)}), f32[4096,128]{0,1:T(8,128)}) %all-reduce.13.cloned.1.call-update) | async-done | bytes 2097168 | tf_op jit(solution)/shard_map/psum | solution.py:125
  395.6 20.3 %all_to_all.31 = f32[32,32,128]{2,1,0:T(8,128)S(1)} all-to-all(f32[32,32,128]{2,1,0:T(8,128)S(1)} %broadcast_select_fusion.2), channel_id=1, replica_groups=mesh['row'=4,'col'=8] {'row','col'}, dimensions={0} | all-to-all | bytes 1048576 | tf_op jit(solution)/shard_map/all_to_all | solution.py:97
  417.0 36.1 %all-reduce.15.cloned.1.call-done = f32[2048,128]{0,1:T(8,128)} async-done(((f32[2048,128]{0,1:T(8,128)}), f32[2048,128]{0,1:T(8,128)}) %all-reduce.15.cloned.1.call-update) | async-done | bytes 1048592 | tf_op jit(solution)/shard_map/psum | solution.py:20
  453.1 39.1 %fusion.31 = f32[128,4096]{1,0:T(8,128)} fusion(f32[2048,128]{0,1:T(8,128)} %all-reduce.15.cloned.1.call-done, f32[4096,2048]{1,0:T(8,128)} %param.21), kind=kOutput, calls=%fused_computation.108 | convolution fusion | flops 12884901888 | bytes 36700160 | tf_op jit(solution)/shard_map/dot_general | solution.py:119
  500.2 4.6 all-to-all-start.5
  511.9 9.5 %all-to-all-done.5 = f32[32,32,128]{2,1,0:T(8,128)S(1)} async-done(((f32[32,32,128]{2,1,0:T(8,128)}), f32[32,32,128]{2,1,0:T(8,128)S(1)}, u32[]{:S(2)}, u32[]{:S(2)}) %all-to-all-start.5) | async-done | bytes 524320 | tf_op jit(solution)/shard_map/all_to_all | solution.py:100
  521.6 8.2 %scatter_custom_fusion.2 = f32[4096,128]{1,0:T(8,128)} fusion(s32[1024]{0:T(1024)S(1)} %bitcast.134, f32[1024,128]{1,0:T(8,128)S(1)} %bitcast.122, f32[]{:T(128)} %constant.143.clone.1), kind=kCustom, calls=%fused_computation.40 | custom fusion | flops 131072 | bytes 2097156 | tf_op jit(solution)/shard_map/scatter-add | solution.py:107
  529.8 10.7 %fusion.3 = f32[8,512,128]{2,1,0:T(8,128)} fusion(f32[8,512,128]{2,1,0:T(8,128)S(1)} %fusion.20, f32[8,512,128]{2,1,0:T(8,128)} %bitcast.110, f32[8,512,512]{2,1,0:T(8,128)} %param.22), kind=kOutput, calls=%fused_computation.21 | convolution fusion | flops 3223322624 | bytes 14680064 | tf_op jit(solution)/shard_map/enm,emr->enr/dot_general | solution.py:127
  542.2 47.5 %all-reduce.17.cloned.1.call-done = f32[4096,128]{0,1:T(8,128)} async-done(((f32[4096,128]{0,1:T(8,128)}), f32[4096,128]{0,1:T(8,128)}) %all-reduce.17.cloned.1.call-update) | async-done | bytes 2097168 | tf_op jit(solution)/shard_map/psum | solution.py:125
  (143 shorter events, 94.2 us)
Async XLA Ops:
  7.2 62.0 %all-reduce.7.cloned.1.call-start = ((), (), s32[]{:S(2)}) async-start(), calls=%async_computation.6 | async-start | bytes 2097152 | tf_op jit(solution)/shard_map/psum | solution.py:20
  10.1 2.5 copy-start.8
  10.1 2.5 copy-start.9
  10.1 5.5 copy-start.10
  10.1 6.9 %copy-start.1 = (f32[8,512,128]{2,1,0:T(8,128)S(1)}, f32[8,512,128]{2,1,0:T(8,128)}, u32[]{:S(2)}) copy-start(f32[8,512,128]{2,1,0:T(8,128)} %param.18) | copy-start | bytes 6291460
  19.8 13.8 %copy-start.7 = (f32[512,128]{1,0:T(8,128)S(1)}, f32[512,128]{1,0:T(8,128)}, u32[]{:S(2)}) copy-start(f32[512,128]{1,0:T(8,128)} %param.20) | copy-start | bytes 786436
  19.8 15.4 %copy-start.11 = (s32[16384]{0:T(1024)S(1)}, s32[16384]{0:T(1024)}, u32[]{:S(2)}) copy-start(s32[16384]{0:T(1024)} %param.26) | copy-start | bytes 196612
  20.9 23.9 %all-to-all-start = ((f32[32,32,128]{2,1,0:T(8,128)}), f32[32,32,128]{2,1,0:T(8,128)S(1)}, u32[]{:S(2)}, u32[]{:S(2)}) async-start(f32[32,32,128]{2,1,0:T(8,128)} %broadcast_select_fusion.8), calls=%async_computation | async-start | bytes 1048576 | tf_op jit(solution)/shard_map/all_to_all | solution.py:97
  28.9 92.0 %collective-permute-start = (f32[8,64,128]{2,1,0:T(8,128)}, f32[8,64,128]{2,1,0:T(8,128)S(1)}, u32[]{:S(2)}, u32[]{:S(2)}) collective-permute-start(f32[8,64,128]{2,1,0:T(8,128)} %slice.98), channel_id=1, source_target_pairs={{0,1},{1,2},{2,3},{3,4},{4,5},{5,6},{6,7},{7,8},{8,9},{9,10},{10,1... | collective-permute-start | bytes 786440 | tf_op jit(solution)/shard_map/ppermute | solution.py:15
  109.3 1.3 copy-start.5
  113.6 6.5 %copy-start.13 = (s32[8,64]{1,0:T(8,128)S(1)}, s32[8,64]{1,0:T(8,128)}, u32[]{:S(2)}) copy-start(s32[8,64]{1,0:T(8,128)} %param.27) | copy-start | bytes 6148
  114.6 20.9 %all-to-all-start.1 = ((f32[32,32,128]{2,1,0:T(8,128)}), f32[32,32,128]{2,1,0:T(8,128)S(1)}, u32[]{:S(2)}, u32[]{:S(2)}) async-start(f32[32,32,128]{2,1,0:T(8,128)} %broadcast_select_fusion.7), calls=%async_computation.1 | async-start | bytes 1048576 | tf_op jit(solution)/shard_map/all_to_all | solution.py:100
  119.2 72.0 %all-reduce.9.cloned.1.call-start = ((), (), s32[]{:S(2)}) async-start(), calls=%async_computation.7 | async-start | bytes 4194304 | tf_op jit(solution)/shard_map/psum | solution.py:125
  124.6 129.2 %all-reduce.11.cloned.1.call-start = ((), (), s32[]{:S(2)}) async-start(), calls=%async_computation.8 | async-start | bytes 2097152 | tf_op jit(solution)/shard_map/psum | solution.py:20
  155.0 150.7 %copy-start = (f32[8,512,128]{2,1,0:T(8,128)}, f32[8,512,128]{2,1,0:T(8,128)S(1)}, u32[]{:S(2)}) copy-start(f32[8,512,128]{2,1,0:T(8,128)S(1)} %fusion.21) | copy-start | bytes 6291460
  295.8 1.3 copy-start.6
  301.0 21.2 %all-to-all-start.3 = ((f32[32,32,128]{2,1,0:T(8,128)}), f32[32,32,128]{2,1,0:T(8,128)S(1)}, u32[]{:S(2)}, u32[]{:S(2)}) async-start(f32[32,32,128]{2,1,0:T(8,128)} %broadcast_select_fusion.4), calls=%async_computation.3 | async-start | bytes 1048576 | tf_op jit(solution)/shard_map/all_to_all | solution.py:100
  305.6 84.9 %all-reduce.13.cloned.1.call-start = ((), (), s32[]{:S(2)}) async-start(), calls=%async_computation.9 | async-start | bytes 4194304 | tf_op jit(solution)/shard_map/psum | solution.py:125
  305.7 3.3 collective-permute-start.1
  312.7 140.4 %all-reduce.15.cloned.1.call-start = ((), (), s32[]{:S(2)}) async-start(), calls=%async_computation.10 | async-start | bytes 2097152 | tf_op jit(solution)/shard_map/psum | solution.py:20
  393.0 1.3 copy-start.2
  500.2 21.2 %all-to-all-start.5 = ((f32[32,32,128]{2,1,0:T(8,128)}), f32[32,32,128]{2,1,0:T(8,128)S(1)}, u32[]{:S(2)}, u32[]{:S(2)}) async-start(f32[32,32,128]{2,1,0:T(8,128)} %broadcast_select_fusion.1), calls=%async_computation.5 | async-start | bytes 1048576 | tf_op jit(solution)/shard_map/all_to_all | solution.py:100
  504.8 84.9 %all-reduce.17.cloned.1.call-start = ((), (), s32[]{:S(2)}) async-start(), calls=%async_computation.11 | async-start | bytes 4194304 | tf_op jit(solution)/shard_map/psum | solution.py:125
  504.9 3.3 collective-permute-start.2
  (3 other events, 3.3 us)
Sparse Core Ops, SparseCore 0:
  12.7 56.4 all-reduce.6
  124.8 66.3 all-reduce.8
  196.2 57.6 all-reduce.10
  312.9 77.6 all-reduce.12
  395.5 57.5 all-reduce.14
  512.0 77.6 all-reduce.16
where the time goes:
time: 605 us; the launch traced here: 601 us
  waiting for transfers between devices  263 us (43%)
  matrix products  150 us (25%)
  other arithmetic  55 us (9%)
  local copies, waits for them, and re-layouts  49 us (8%)
  blocking collectives  40.9 us (7%)
  starting transfers between devices  28.6 us (5%)
  between operations  15.1 us (2%)
    psum x3, waiting for transfers between devices, shards(): residual = lax.psum(partial_value, 'col')  127 us
    dot_general x3, matrix products, shards(): jnp.dot(kernel, column_values, precision=highest, preferred_element_type=...  117 us
    psum x3, waiting for transfers between devices, spread(): return lax.psum(block, axis)  95.1 us
    all_to_all x2, blocking collectives, shards(): lax.all_to_all(outgoing, ('row', 'col'), split_axis=0, concat_axis=0, til...  40.9 us
    dot_general x3, matrix products, shards(): jnp.einsum('enm,emr->enr', elem_mats, volume_field, precision=highest)  32.8 us
    all_to_all x3, waiting for transfers between devices, shards(): lax.all_to_all(leaving, ('row', 'col'), split_axis=0, concat_axis=0, tile...  29.7 us
    scatter-add x3, other arithmetic, shards(): flux_field = jnp.zeros_like(volume_flat).at[flux_take.reshape(-1)].add(la...  24.3 us
    unnamed x35, local copies, waits for them, and re-layouts  15.8 us
  transfers between devices with their start and end apart: 13, of which 12 were waited for; matrix products, arithmetic and copies ran while one was open for 23% of the time, Pallas kernels for 0%

commit v1 on v0

--- a/solution.py
+++ b/solution.py
@@ -122,7 +122,7 @@
         row_start = col_index * share_rows
         own_part = lax.dynamic_slice_in_dim(partial_value, row_start, share_rows, 0) + local_term
         partial_value = lax.dynamic_update_slice_in_dim(partial_value, own_part, row_start, 0)
-        residual = lax.psum(partial_value, "col")
+        residual = jnp.sum(lax.all_gather(partial_value, "col"), axis=0)
         panel_current = panel_current - boundary_step * residual
         applied = jnp.einsum("enm,emr->enr", elem_mats, volume_field, precision=highest)
         updated = volume_field - volume_step * (volume_field + applied - flux_field)

time: 605 us -> 919 us (1.52)
  waiting for transfers between devices: 263 us -> 507 us
  other arithmetic: 55 us -> 88 us
  local copies, waits for them, and re-layouts: 49 us -> 76.6 us
    all_gather x0 -> x3, waiting for transfers between devices: none -> 425 us  [shards(): residual = jnp.sum(lax.all_gather(partial_value, 'col'), axis=0)]
    psum x3 -> x0, waiting for transfers between devices: 127 us -> none  [shards(): residual = lax.psum(partial_value, 'col')]
    all_to_all x3 -> x2, waiting for transfers between devices: 29.7 us -> 5.08 us  [shards(): lax.all_to_all(leaving, ('row', 'col'), split_axis=0, concat_axis=0, tile...]
    reduce_sum x0 -> x3, other arithmetic: none -> 24.4 us  [shards(): residual = jnp.sum(lax.all_gather(partial_value, 'col'), axis=0)]
    all_to_all x2 -> x1, blocking collectives: 40.9 us -> 18.8 us  [shards(): lax.all_to_all(outgoing, ('row', 'col'), split_axis=0, concat_axis=0, til...]
    psum x3, waiting for transfers between devices: 95.1 us -> 75.3 us  [spread(): return lax.psum(block, axis)]
    all_to_all x0 -> x1, blocking collectives: none -> 18.8 us  [shards(): lax.all_to_all(leaving, ('row', 'col'), split_axis=0, concat_axis=0, tile...]
    all_to_all x1 -> x2, starting transfers between devices: 7.33 us -> 16.9 us  [shards(): lax.all_to_all(outgoing, ('row', 'col'), split_axis=0, concat_axis=0, til...]
  transfers between devices with their start and end apart: 13 -> 13, of which waited for: 12 -> 8; matrix products, arithmetic and copies ran while one was open for 23% -> 21% of each run, Pallas kernels for 0% -> 0%
where the time goes in v1:
time: 919 us; the launch traced here: 910 us
  waiting for transfers between devices  507 us (55%)
  matrix products  152 us (17%)
  other arithmetic  88 us (10%)
  local copies, waits for them, and re-layouts  76.6 us (8%)
  blocking collectives  37.6 us (4%)
  starting transfers between devices  34.3 us (4%)
  between operations  15.1 us (2%)
    all_gather x3, waiting for transfers between devices, shards(): residual = jnp.sum(lax.all_gather(partial_value, 'col'), axis=0)  425 us
    dot_general x3, matrix products, shards(): jnp.dot(kernel, column_values, precision=highest, preferred_element_type=...  117 us
    psum x3, waiting for transfers between devices, spread(): return lax.psum(block, axis)  75.3 us
    dot_general x3, matrix products, shards(): jnp.einsum('enm,emr->enr', elem_mats, volume_field, precision=highest)  34.3 us
    scatter-add x3, other arithmetic, shards(): flux_field = jnp.zeros_like(volume_flat).at[flux_take.reshape(-1)].add(la...  24.5 us
    reduce_sum x3, other arithmetic, shards(): residual = jnp.sum(lax.all_gather(partial_value, 'col'), axis=0)  24.4 us
    unnamed x37, local copies, waits for them, and re-layouts  19.9 us
    all_to_all x1, blocking collectives, shards(): lax.all_to_all(outgoing, ('row', 'col'), split_axis=0, concat_axis=0, til...  18.8 us
  transfers between devices with their start and end apart: 13, of which 8 were waited for; matrix products, arithmetic and copies ran while one was open for 21% of the time, Pallas kernels for 0%

profile of v1, /device:TPU:0, one launch (start us, length us, event | category | flops | bytes accessed | tf_op | source)
XLA Modules:
  0.0 910.1 jit_solution(1967651826180414449)
XLA Ops:
  19.9 7.3 all-to-all-start.1
  48.4 8.1 scatter_custom_fusion
  56.5 11.2 %multiply_subtract_fusion.2 = f32[8,512,128]{2,1,0:T(8,128)S(1)} fusion(f32[8,512,128]{2,1,0:T(8,128)} %param.18, f32[8,512,128]{2,1,0:T(8,128)} %bitcast.124, f32[8,512,512]{2,1,0:T(8,128)} %param.22), kind=kOutput, calls=%fused_computation.28 | convolution fusion | flops 3223322624 | bytes 14680064 | tf_op jit(solution)/shard_map/enm,emr->enr/dot_general | solution.py:127
  71.9 5.8 all-to-all-start
  77.7 13.8 %all-reduce.4.cloned.1.call-done = f32[2048,128]{0,1:T(8,128)} async-done(((f32[2048,128]{0,1:T(8,128)}), f32[2048,128]{0,1:T(8,128)}) %all-reduce.4.cloned.1.call-update) | async-done | bytes 1048592 | tf_op jit(solution)/shard_map/psum | solution.py:20
  91.5 39.1 %fusion.26 = f32[128,4096]{1,0:T(8,128)} fusion(f32[2048,128]{0,1:T(8,128)} %all-reduce.4.cloned.1.call-done, f32[4096,2048]{1,0:T(8,128)} %param.21), kind=kOutput, calls=%fused_computation.106 | convolution fusion | flops 12884901888 | bytes 36700160 | tf_op jit(solution)/shard_map/dot_general | solution.py:119
  140.1 151.4 %all-gather.4.cloned.1.call-done = f32[8,4096,128]{2,1,0:T(8,128)} async-done(((f32[1,4096,128]{2,1,0:T(8,128)}), f32[8,4096,128]{2,1,0:T(8,128)}) %all-gather.4.cloned.1.call-update) | async-done | bytes 16777232 | tf_op jit(solution)/shard_map/all_gather | solution.py:125
  291.4 8.1 reduce_sum.82
  307.5 18.8 %all_to_all.30 = f32[32,32,128]{2,1,0:T(8,128)S(1)} all-to-all(f32[32,32,128]{2,1,0:T(8,128)S(1)} %copy-done.8), channel_id=1, replica_groups=mesh['row'=4,'col'=8] {'row','col'}, dimensions={0} | all-to-all | bytes 1048576 | tf_op jit(solution)/shard_map/all_to_all | solution.py:97
  327.5 36.1 %all-reduce.6.cloned.1.call-done = f32[2048,128]{0,1:T(8,128)} async-done(((f32[2048,128]{0,1:T(8,128)}), f32[2048,128]{0,1:T(8,128)}) %all-reduce.6.cloned.1.call-update) | async-done | bytes 1048592 | tf_op jit(solution)/shard_map/psum | solution.py:20
  363.5 39.2 %fusion.27 = f32[128,4096]{1,0:T(8,128)} fusion(f32[2048,128]{0,1:T(8,128)} %all-reduce.6.cloned.1.call-done, f32[4096,2048]{1,0:T(8,128)} %param.21), kind=kOutput, calls=%fused_computation.107 | convolution fusion | flops 12884901888 | bytes 36700160 | tf_op jit(solution)/shard_map/dot_general | solution.py:119
  414.6 147.3 %all-gather.6.cloned.1.call-done = f32[8,4096,128]{2,1,0:T(8,128)} async-done(((f32[1,4096,128]{2,1,0:T(8,128)}), f32[8,4096,128]{2,1,0:T(8,128)}) %all-gather.6.cloned.1.call-update) | async-done | bytes 16777232 | tf_op jit(solution)/shard_map/all_gather | solution.py:125
  561.8 8.1 reduce_sum.87
  582.9 18.8 %all_to_all.31 = f32[32,32,128]{2,1,0:T(8,128)S(1)} all-to-all(f32[32,32,128]{2,1,0:T(8,128)S(1)} %get-tuple-element.51), channel_id=1, replica_groups=mesh['row'=4,'col'=8] {'row','col'}, dimensions={0} | all-to-all | bytes 1048576 | tf_op jit(solution)/shard_map/all_to_all | solution.py:100
  608.4 6.0 gather_fusion.10
  623.6 8.0 scatter_custom_fusion.1
  631.6 11.2 %fusion.6 = f32[8,512,128]{2,1,0:T(8,128)S(1)} fusion(f32[8,512,128]{2,1,0:T(8,128)} %copy-done, f32[8,512,128]{2,1,0:T(8,128)} %bitcast.123, f32[8,512,512]{2,1,0:T(8,128)} %param.22), kind=kOutput, calls=%fused_computation.25 | convolution fusion | flops 3223322624 | bytes 14680064 | tf_op jit(solution)/shard_map/enm,emr->enr/dot_general | solution.py:127
  646.7 11.2 %all-to-all-start.4 = ((f32[32,32,128]{2,1,0:T(8,128)}), f32[32,32,128]{2,1,0:T(8,128)S(1)}, u32[]{:S(2)}, u32[]{:S(2)}) async-start(f32[32,32,128]{2,1,0:T(8,128)} %broadcast_select_fusion.2), calls=%async_computation.4 | async-start | bytes 1048576 | tf_op jit(solution)/shard_map/all_to_all | solution.py:97
  658.1 25.4 %all-reduce.8.cloned.1.call-done = f32[2048,128]{0,1:T(8,128)} async-done(((f32[2048,128]{0,1:T(8,128)}), f32[2048,128]{0,1:T(8,128)}) %all-reduce.8.cloned.1.call-update) | async-done | bytes 1048592 | tf_op jit(solution)/shard_map/psum | solution.py:20
  683.5 39.1 %fusion.28 = f32[128,4096]{1,0:T(8,128)} fusion(f32[2048,128]{0,1:T(8,128)} %all-reduce.8.cloned.1.call-done, f32[4096,2048]{1,0:T(8,128)} %param.21), kind=kOutput, calls=%fused_computation.108 | convolution fusion | flops 12884901888 | bytes 36700160 | tf_op jit(solution)/shard_map/dot_general | solution.py:119
  731.8 8.4 scatter_custom_fusion.2
  741.9 11.9 %fusion.3 = f32[8,512,128]{2,1,0:T(8,128)} fusion(f32[8,512,128]{2,1,0:T(8,128)S(1)} %fusion.20, f32[8,512,128]{2,1,0:T(8,128)} %bitcast.122, f32[8,512,512]{2,1,0:T(8,128)} %param.22), kind=kOutput, calls=%fused_computation.21 | convolution fusion | flops 3223322624 | bytes 14680064 | tf_op jit(solution)/shard_map/enm,emr->enr/dot_general | solution.py:127
  759.1 126.6 %all-gather.8.cloned.1.call-done = f32[8,4096,128]{2,1,0:T(8,128)} async-done(((f32[1,4096,128]{2,1,0:T(8,128)}), f32[8,4096,128]{2,1,0:T(8,128)}) %all-gather.8.cloned.1.call-update) | async-done | bytes 16777232 | tf_op jit(solution)/shard_map/all_gather | solution.py:125
  885.8 8.2 reduce_sum.88
  (154 shorter events, 126.0 us)
Async XLA Ops:
  14.6 1.3 copy-start.6
  18.9 8.4 copy-start.1
  19.9 28.2 %all-to-all-start.1 = ((f32[32,32,128]{2,1,0:T(8,128)}), f32[32,32,128]{2,1,0:T(8,128)S(1)}, u32[]{:S(2)}, u32[]{:S(2)}) async-start(f32[32,32,128]{2,1,0:T(8,128)} %broadcast_select_fusion.7), calls=%async_computation.1 | async-start | bytes 1048576 | tf_op jit(solution)/shard_map/all_to_all | solution.py:100
  27.3 5.6 copy-start.9
  27.3 5.6 copy-start.10
  27.3 64.2 %all-reduce.4.cloned.1.call-start = ((), (), s32[]{:S(2)}) async-start(), calls=%async_computation.6 | async-start | bytes 2097152 | tf_op jit(solution)/shard_map/psum | solution.py:20
  28.1 6.5 copy-start.11
  28.1 16.4 %collective-permute-start = (f32[8,64,128]{2,1,0:T(8,128)}, f32[8,64,128]{2,1,0:T(8,128)S(1)}, u32[]{:S(2)}, u32[]{:S(2)}) collective-permute-start(f32[8,64,128]{2,1,0:T(8,128)} %slice.98), channel_id=1, source_target_pairs={{0,1},{1,2},{2,3},{3,4},{4,5},{5,6},{6,7},{7,8},{8,9},{9,10},{10,1... | collective-permute-start | bytes 786440 | tf_op jit(solution)/shard_map/ppermute | solution.py:15
  30.4 5.5 copy-start.14
  30.4 7.1 copy-start.12
  67.8 537.3 %copy-start = (f32[8,512,128]{2,1,0:T(8,128)}, f32[8,512,128]{2,1,0:T(8,128)S(1)}, u32[]{:S(2)}) copy-start(f32[8,512,128]{2,1,0:T(8,128)S(1)} %fusion.21) | copy-start | bytes 6291460
  67.8 2.8 copy-start.7
  71.9 62.0 %all-to-all-start = ((f32[32,32,128]{2,1,0:T(8,128)}), f32[32,32,128]{2,1,0:T(8,128)S(1)}, u32[]{:S(2)}, u32[]{:S(2)}) async-start(f32[32,32,128]{2,1,0:T(8,128)} %get-tuple-element.53), calls=%async_computation | async-start | bytes 1048576 | tf_op jit(solution)/shard_map/all_to_all | solution.py:97
  77.7 213.8 %all-gather.4.cloned.1.call-start = ((), (), s32[]{:S(2)}) async-start(), calls=%async_computation.7 | async-start | bytes 18874368 | tf_op jit(solution)/shard_map/all_gather | solution.py:125
  139.8 223.7 %all-reduce.6.cloned.1.call-start = ((), (), s32[]{:S(2)}) async-start(), calls=%async_computation.8 | async-start | bytes 2097152 | tf_op jit(solution)/shard_map/psum | solution.py:20
  307.3 254.5 %all-gather.6.cloned.1.call-start = ((), (), s32[]{:S(2)}) async-start(), calls=%async_computation.9 | async-start | bytes 18874368 | tf_op jit(solution)/shard_map/all_gather | solution.py:125
  601.7 19.9 %all-to-all-start.5 = ((f32[32,32,128]{2,1,0:T(8,128)}), f32[32,32,128]{2,1,0:T(8,128)}, u32[]{:S(2)}, u32[]{:S(2)}) async-start(f32[32,32,128]{2,1,0:T(8,128)} %get-tuple-element.50), calls=%async_computation.5 | async-start | bytes 1048576 | tf_op jit(solution)/shard_map/all_to_all | solution.py:100
  605.0 78.4 %all-reduce.8.cloned.1.call-start = ((), (), s32[]{:S(2)}) async-start(), calls=%async_computation.10 | async-start | bytes 2097152 | tf_op jit(solution)/shard_map/psum | solution.py:20
  605.1 10.2 %copy-start.3 = (f32[4096,128]{0,1:T(8,128)S(1)}, f32[4096,128]{0,1:T(8,128)}, u32[]{:S(2)}) copy-start(f32[4096,128]{0,1:T(8,128)} %copy-done.2) | copy-start | bytes 6291460
  605.1 3.2 collective-permute-start.1
  646.7 79.1 %all-to-all-start.4 = ((f32[32,32,128]{2,1,0:T(8,128)}), f32[32,32,128]{2,1,0:T(8,128)S(1)}, u32[]{:S(2)}, u32[]{:S(2)}) async-start(f32[32,32,128]{2,1,0:T(8,128)} %broadcast_select_fusion.2), calls=%async_computation.4 | async-start | bytes 1048576 | tf_op jit(solution)/shard_map/all_to_all | solution.py:97
  657.9 227.9 %all-gather.8.cloned.1.call-start = ((), (), s32[]{:S(2)}) async-start(), calls=%async_computation.11 | async-start | bytes 18874368 | tf_op jit(solution)/shard_map/all_gather | solution.py:125
  740.2 13.5 %collective-permute-start.2 = (f32[8,64,128]{2,1,0:T(8,128)S(1)}, f32[8,64,128]{2,1,0:T(8,128)S(1)}, u32[]{:S(2)}, u32[]{:S(2)}) collective-permute-start(f32[8,64,128]{2,1,0:T(8,128)S(1)} %slice.133), channel_id=1, source_target_pairs={{0,1},{1,2},{2,3},{3,4},{4,5},{5,6},{6,7},{7,8},{8,9},{9,10},{10,1... | collective-permute-start | bytes 786440 | tf_op jit(solution)/shard_map/ppermute | solution.py:15
  894.0 3.1 copy-start.4
  (4 other events, 5.0 us)
Sparse Core Ops, SparseCore 0:
  33.0 58.5 all-reduce.3
  139.9 151.4 all-gather.3
  307.5 56.0 all-reduce.5
  410.7 151.0 all-gather.5
  616.6 66.8 all-reduce.7
  731.9 153.8 all-gather.7
